TPU v7x, 32 devices: a whole 2x2x4 slice. The times are simulated.
32 devices in a mesh: island: 8 (over y, x, core), fsdp: 4 (over z).
Axes of the slice: x: 2, y: 2, z: 4, core: 2. Of those that a mesh axis runs over, the one named last changes fastest.
Arguments:
- tokens: bfloat16 [8, 1024, 8192], P('island', 'fsdp'), may hold values from -6 to 6
- cotangent: bfloat16 [8, 1024, 1024], P('island', 'fsdp'), may hold values from -0.1875 to 0.1875
- params: float32 [8, 8192, 1024], P('island', 'fsdp'), may hold values from -0.18 to 0.18
- first_moment: bfloat16 [8, 8192, 1024], P('island', 'fsdp'), may hold values from -3 to 3
- second_moment: bfloat16 [8, 8192, 1024], P('island', 'fsdp'), may hold values from 0.25 to 4
- base: float32 [8192, 512], P(('fsdp', 'island')), may hold values from -0.18 to 0.18
- outer_momentum: float32 [8192, 512], P(('fsdp', 'island')), may hold values from -0.06 to 0.06
- head_order: int32 [8], replicated, may hold values from 0 to 7, each once
- step_fragment: int32 [1], replicated, may hold values from 0 to 1
Outputs:
- params_out: float32 [8, 8192, 1024], P('island', 'fsdp')
- first_out: bfloat16 [8, 8192, 1024], P('island', 'fsdp')
- second_out: bfloat16 [8, 8192, 1024], P('island', 'fsdp')
- base_out: float32 [8192, 512], P(('fsdp', 'island'))
- momentum_out: float32 [8192, 512], P(('fsdp', 'island'))
All inputs are finite; a program needn't handle non-finite values.
Results may differ from a plain program's by a relative error of at most 0.012.
Values may be sent and summed in bfloat16 or wider, within the bound.
No kernel may reach another device: no remote copies, remote signals or barrier semaphores. Data moves between devices by JAX's collectives and lax.ppermute only.
A program may use at most 128 MiB of HBM per device.

v0:
```python
import jax
import jax.numpy as jnp
from jax import lax
from jax.sharding import PartitionSpec as P

KVH = 8
HD = 128
SYNC = 4


def outer_update(base, outer_momentum, total, islands):
    delta = base - total / islands
    momentum = 0.9 * outer_momentum + delta
    return (base - 0.7 * (delta + 0.9 * momentum), momentum)


def shards(
    tokens,
    cotangent,
    params,
    first_moment,
    second_moment,
    base,
    outer_momentum,
    head_order,
    step_fragment,
):
    local_tokens = tokens[0]
    weights = params[0]
    rows = weights.shape[0]
    width = weights.shape[1]
    block = local_tokens.shape[0]
    columns = lax.all_to_all(tokens, "fsdp", split_axis=2, concat_axis=1, tiled=True)[0]
    piece = lax.all_gather(cotangent, "fsdp", axis=1, tiled=True)
    blocks = piece.shape[1] // block

    def one_block(index, running):
        grads_part = lax.dynamic_slice_in_dim(piece[0], index * block, block, 0)
        token_part = lax.dynamic_slice_in_dim(columns, index * block, block, 0)
        part = lax.dot_general(
            token_part, grads_part, (((0,), (0,)), ((), ())), preferred_element_type=jnp.float32
        )
        part = lax.optimization_barrier(part.astype(jnp.bfloat16)).astype(jnp.float32)
        return running + part

    grad = lax.fori_loop(0, blocks, one_block, jnp.zeros((rows, width), jnp.float32))
    moment_one = 0.9 * first_moment[0].astype(jnp.float32) + 0.1 * grad
    moment_two = 0.95 * second_moment[0].astype(jnp.float32) + 0.05 * grad * grad
    stepped = weights - 0.01 * (moment_one / (jnp.sqrt(moment_two) + 1e-08) + 0.1 * weights)
    heads = lax.dynamic_slice(head_order, (step_fragment[0] * SYNC,), (SYNC,))
    shaped = stepped.reshape(rows, KVH, HD)
    fragment = jnp.take(shaped, heads, axis=1).reshape(rows, SYNC * HD)
    islands = lax.axis_size("island")
    total = lax.psum_scatter(
        fragment.astype(jnp.bfloat16), "island", scatter_dimension=0, tiled=True
    ).astype(jnp.float32)
    base_next, momentum_next = outer_update(base, outer_momentum, total, islands)
    whole_base = lax.all_gather(
        base_next.astype(jnp.bfloat16), "island", axis=0, tiled=True
    ).astype(base_next.dtype)
    updated = shaped.at[:, heads, :].set(whole_base.reshape(rows, SYNC, HD)).reshape(rows, width)
    return (
        updated[None],
        moment_one.astype(jnp.bfloat16)[None],
        moment_two.astype(jnp.bfloat16)[None],
        base_next,
        momentum_next,
    )


def solution(mesh):
    placed = (
        P("island", "fsdp", None),
        P("island", "fsdp", None),
        P("island", "fsdp", None),
        P("island", "fsdp", None),
        P("island", "fsdp", None),
        P(("fsdp", "island"), None),
        P(("fsdp", "island"), None),
        P(),
        P(),
    )
    return jax.shard_map(
        shards,
        mesh=mesh,
        in_specs=placed,
        out_specs=(
            P("island", "fsdp", None),
            P("island", "fsdp", None),
            P("island", "fsdp", None),
            P(("fsdp", "island"), None),
            P(("fsdp", "island"), None),
        ),
        check_vma=False,
    )
```

profile of v0, /device:TPU:0, one launch (start us, length us, event | category | flops | bytes accessed | tf_op | source)
XLA Modules:
  0.0 422.3 jit_solution(16253507385062909303)
XLA Ops:
  7.2 17.8 %copy.73 = bf16[1,256,8192]{1,0,2:T(2,128)(2,1)} copy(bf16[1,256,8192]{2,1,0:T(8,128)(2,1)} %param.11) | data formatting | bytes 8388608 | tf_op args[0]
  25.4 43.5 %reduce = bf16[8192,256]{1,0:T(8,128)(2,1)} reduce(bf16[8192,1,256]{2,1,0:T(2,128)(2,1)} %bitcast.56, bf16[]{:T(256)} %broadcast.57), dimensions={1}, to_apply=%bitcast.50.reduce_sub_computation | reduce | bytes 8388610
  69.0 5.1 %reshape.62 = bf16[4,2,262144]{2,1,0:T(2,128)(2,1)} reshape(bf16[8192,256]{1,0:T(8,128)(2,1)} %reduce) | data formatting | bytes 8388608
  74.1 6.3 %all-to-all-start = ((bf16[4,2,262144]{2,1,0:T(2,128)(2,1)}), bf16[4,2,262144]{2,1,0:T(2,128)(2,1)}, u32[]{:S(2)}, u32[]{:S(2)}) async-start(bf16[4,2,262144]{2,1,0:T(2,128)(2,1)} %reshape.62), calls=%async_computation | async-start | bytes 8388608 | tf_op jit(solution)/shard_map/all_to_all | solution.py:33
  82.0 9.3 %copy.71 = f32[1,2048,1024]{1,2,0:T(8,128)} copy(f32[1,2048,1024]{2,1,0:T(8,128)} %param.13) | data formatting | bytes 16777216 | tf_op args[2]
  91.3 6.6 %copy.72 = bf16[1,2048,1024]{1,2,0:T(8,128)(2,1)} copy(bf16[1,2048,1024]{2,1,0:T(8,128)(2,1)} %param.14) | data formatting | bytes 8388608 | tf_op args[3]
  97.9 6.5 %copy.76 = bf16[1,2048,1024]{1,2,0:T(8,128)(2,1)} copy(bf16[1,2048,1024]{2,1,0:T(8,128)(2,1)} %param.15) | data formatting | bytes 8388608 | tf_op args[4]
  104.6 103.0 %all-to-all-done = bf16[4,2,262144]{2,1,0:T(2,128)(2,1)} async-done(((bf16[4,2,262144]{2,1,0:T(2,128)(2,1)}), bf16[4,2,262144]{2,1,0:T(2,128)(2,1)}, u32[]{:S(2)}, u32[]{:S(2)}) %all-to-all-start) | async-done | bytes 4194336 | tf_op jit(solution)/shard_map/all_to_all | solution.py:33
  207.6 7.4 %reshape.63 = bf16[8192,1,256]{2,1,0:T(2,128)(2,1)} reshape(bf16[4,2,262144]{2,1,0:T(2,128)(2,1)} %all-to-all-done) | data formatting | bytes 8388608
  215.0 6.1 %copy.90 = bf16[1,256,8192]{1,2,0:T(8,128)(2,1)} copy(bf16[1,256,8192]{1,0,2:T(2,128)(2,1)} %bitcast.57) | data formatting | bytes 8388608
  221.1 6.2 %copy.74 = bf16[1,4,256,2048]{3,2,1,0:T(8,128)(2,1)} copy(bf16[1,4,256,2048]{2,3,1,0:T(8,128)(2,1)} %bitcast.60) | data formatting | bytes 8388608 | tf_op jit(solution)/shard_map/all_to_all | solution.py:33
  227.3 57.0 %while.14 = (s32[]{:T(128)}, f32[2048,1024]{1,0:T(8,128)}, bf16[1024,2048]{1,0:T(8,128)(2,1)}, bf16[1,1024,1024]{2,1,0:T(8,128)(2,1)}, s32[]{:T(128)}, /*index=5*/s32[]{:T(128)}, s32[]{:T(128)}, s32[]{:T(128)}) while((s32[]{:T(128)}, f32[2048,1024]{1,0:T(8,128)}, bf16[1024,2048]{1,0:T(8,128)(2,1)}, ...), condition=%wide.region_1.0_spmd.clone, body=%wide.region_0.0_spmd.clone.sunk | while | flops 1082130432 | bytes 26739852 | solution.py:46
  227.3 4.7 %convolution_convert_fusion.2 = bf16[2048,1024]{1,0:T(8,128)(2,1)} fusion(bf16[1024,2048]{1,0:T(8,128)(2,1)} %get-tuple-element.179, s32[]{:T(128)S(6)} %select_n.32, bf16[1,1024,1024]{2,1,0:T(8,128)(2,1)} %get-tuple-element.180), kind=kOutput, calls=%fused_computation.3.clone.1 | convolution fusion | flops 1075838976 | bytes 5768192 | tf_op jit(solution)/shard_map/while/body/eval_jaxpr/dot_general | solution.py:40
  231.9 7.8 %select_add_fusion.2 = f32[2048,1024]{1,0:T(8,128)} fusion(f32[2048,1024]{1,0:T(8,128)} %get-tuple-element.170, bf16[2048,1024]{1,0:T(8,128)(2,1)} %convolution_convert_fusion.2, pred[]{:T(512)S(6)} %compare.3), kind=kLoop, calls=%fused_computation.2.clone.1 | loop fusion | flops 6291456 | bytes 20971520 | tf_op jit(solution)/shard_map/while/body/eval_jaxpr/add | solution.py:44
  239.7 4.7 %convolution_convert_fusion.2 = bf16[2048,1024]{1,0:T(8,128)(2,1)} fusion(bf16[1024,2048]{1,0:T(8,128)(2,1)} %get-tuple-element.179, s32[]{:T(128)S(6)} %select_n.32, bf16[1,1024,1024]{2,1,0:T(8,128)(2,1)} %get-tuple-element.180), kind=kOutput, calls=%fused_computation.3.clone.1 | convolution fusion | flops 1075838976 | bytes 5768192 | tf_op jit(solution)/shard_map/while/body/eval_jaxpr/dot_general | solution.py:40
  244.4 10.2 %select_add_fusion.2 = f32[2048,1024]{1,0:T(8,128)} fusion(f32[2048,1024]{1,0:T(8,128)} %get-tuple-element.170, bf16[2048,1024]{1,0:T(8,128)(2,1)} %convolution_convert_fusion.2, pred[]{:T(512)S(6)} %compare.3), kind=kLoop, calls=%fused_computation.2.clone.1 | loop fusion | flops 6291456 | bytes 20971520 | tf_op jit(solution)/shard_map/while/body/eval_jaxpr/add | solution.py:44
  254.6 4.7 %convolution_convert_fusion.2 = bf16[2048,1024]{1,0:T(8,128)(2,1)} fusion(bf16[1024,2048]{1,0:T(8,128)(2,1)} %get-tuple-element.179, s32[]{:T(128)S(6)} %select_n.32, bf16[1,1024,1024]{2,1,0:T(8,128)(2,1)} %get-tuple-element.180), kind=kOutput, calls=%fused_computation.3.clone.1 | convolution fusion | flops 1075838976 | bytes 5768192 | tf_op jit(solution)/shard_map/while/body/eval_jaxpr/dot_general | solution.py:40
  259.3 10.2 %select_add_fusion.2 = f32[2048,1024]{1,0:T(8,128)} fusion(f32[2048,1024]{1,0:T(8,128)} %get-tuple-element.170, bf16[2048,1024]{1,0:T(8,128)(2,1)} %convolution_convert_fusion.2, pred[]{:T(512)S(6)} %compare.3), kind=kLoop, calls=%fused_computation.2.clone.1 | loop fusion | flops 6291456 | bytes 20971520 | tf_op jit(solution)/shard_map/while/body/eval_jaxpr/add | solution.py:44
  269.5 4.7 %convolution_convert_fusion.2 = bf16[2048,1024]{1,0:T(8,128)(2,1)} fusion(bf16[1024,2048]{1,0:T(8,128)(2,1)} %get-tuple-element.179, s32[]{:T(128)S(6)} %select_n.32, bf16[1,1024,1024]{2,1,0:T(8,128)(2,1)} %get-tuple-element.180), kind=kOutput, calls=%fused_computation.3.clone.1 | convolution fusion | flops 1075838976 | bytes 5768192 | tf_op jit(solution)/shard_map/while/body/eval_jaxpr/dot_general | solution.py:40
  274.1 10.2 %select_add_fusion.2 = f32[2048,1024]{1,0:T(8,128)} fusion(f32[2048,1024]{1,0:T(8,128)} %get-tuple-element.170, bf16[2048,1024]{1,0:T(8,128)(2,1)} %convolution_convert_fusion.2, pred[]{:T(512)S(6)} %compare.3), kind=kLoop, calls=%fused_computation.2.clone.1 | loop fusion | flops 6291456 | bytes 20971520 | tf_op jit(solution)/shard_map/while/body/eval_jaxpr/add | solution.py:44
  284.3 9.2 %copy.75 = f32[2048,1024]{0,1:T(8,128)} copy(f32[2048,1024]{1,0:T(8,128)} %get-tuple-element.84) | data formatting | bytes 16777216 | tf_op jit(solution)/shard_map/while | solution.py:46
  293.5 15.2 %fusion.9 = (bf16[1,2048,1024]{1,2,0:T(8,128)(2,1)}, f32[2048,1024]{0,1:T(8,128)}, bf16[1,2048,1024]{1,2,0:T(8,128)(2,1)}) fusion(f32[2048,1024]{0,1:T(8,128)} %copy.75, bf16[1,2048,1024]{1,2,0:T(8,128)(2,1)} %copy.76, bf16[1,2048,1024]{1,2,0:T(8,128)(2,1)} %copy.72, f32[1,2048,1024]{1,2,0:T(8,128)} %copy.71), kind=kLoop, calls=%fused_computation.17 | loop fusion | flops 35651584 | bytes 41943040 | tf_op jit(solution)/shard_map/broadcast_in_dim | solution.py:65
  308.7 4.2 gather_fusion
  315.4 39.6 %reduce-scatter.2.cloned.1.call-done = bf16[256,512]{0,1:T(8,128)(2,1)} async-done(((bf16[2048,512]{0,1:T(8,128)(2,1)}), bf16[256,512]{0,1:T(8,128)(2,1)}) %reduce-scatter.2.cloned.1.call-update) | async-done | bytes 262160 | tf_op jit(solution)/shard_map/reduce_scatter | solution.py:54
  356.9 9.2 %copy.83 = f32[2048,8,128]{2,0,1:T(8,128)} copy(f32[2048,8,128]{0,2,1:T(8,128)} %bitcast.55) | data formatting | bytes 16777216 | tf_op jit(solution)/shard_map/reshape | solution.py:51
  366.1 6.4 %copy.86 = bf16[1,2048,1024]{2,1,0:T(8,128)(2,1)} copy(bf16[1,2048,1024]{1,2,0:T(8,128)(2,1)} %get-tuple-element.134) | data formatting | bytes 8388608
  372.5 6.3 %copy.87 = bf16[1,2048,1024]{2,1,0:T(8,128)(2,1)} copy(bf16[1,2048,1024]{1,2,0:T(8,128)(2,1)} %get-tuple-element.132) | data formatting | bytes 8388608
  380.8 4.4 %all-gather.5.cloned.1.call-done = bf16[2048,512]{0,1:T(8,128)(2,1)} async-done(((bf16[256,512]{0,1:T(8,128)(2,1)}), bf16[2048,512]{0,1:T(8,128)(2,1)}) %all-gather.5.cloned.1.call-update) | async-done | bytes 2097168 | tf_op jit(solution)/shard_map/all_gather | solution.py:58
  385.2 4.1 copy.82
  389.3 8.1 %scatter_fusion = f32[2048,8,128]{2,0,1:T(8,128)} fusion(f32[2048,8,128]{2,0,1:T(8,128)} %copy.83, s32[4]{0:T(128)S(1)} %get-tuple-element.131, f32[4,2048,128]{2,1,0:T(8,128)} %bitcast.61), kind=kCustom, calls=%fused_computation.1 | custom fusion | bytes 12582928 | tf_op jit(solution)/shard_map/scatter | solution.py:61
  397.3 9.2 %copy.84 = f32[2048,8,128]{0,2,1:T(8,128)} copy(f32[2048,8,128]{2,0,1:T(8,128)} %scatter_fusion) | data formatting | bytes 16777216 | tf_op jit(solution)/shard_map/scatter | solution.py:61
  406.6 9.2 %copy.85 = f32[1,2048,1024]{2,1,0:T(8,128)} copy(f32[1,2048,1024]{1,2,0:T(8,128)} %bitcast.58) | data formatting | bytes 16777216
  (24 shorter events, 7.9 us)
Async XLA Ops:
  74.1 133.5 %all-to-all-start = ((bf16[4,2,262144]{2,1,0:T(2,128)(2,1)}), bf16[4,2,262144]{2,1,0:T(2,128)(2,1)}, u32[]{:S(2)}, u32[]{:S(2)}) async-start(bf16[4,2,262144]{2,1,0:T(2,128)(2,1)} %reshape.62), calls=%async_computation | async-start | bytes 8388608 | tf_op jit(solution)/shard_map/all_to_all | solution.py:33
  80.4 146.9 %all-gather.3.cloned.1.call-start = ((), (), s32[]{:S(2)}) async-start(), calls=%async_computation.2 | async-start | bytes 2621440 | tf_op jit(solution)/shard_map/all_gather | solution.py:34
  81.1 273.9 %reduce-scatter.2.cloned.1.call-start = ((), (), s32[]{:S(2)}) async-start(), calls=%async_computation.3 | async-start | bytes 2359296 | tf_op jit(solution)/shard_map/reduce_scatter | solution.py:54
  91.3 13.1 %copy-start.2 = (s32[8]{0:T(128)S(1)}, s32[8]{0:T(128)}, u32[]{:S(2)}) copy-start(s32[8]{0:T(128)} %param.18) | copy-start | bytes 100
  308.7 6.3 %copy-start = (f32[256,512]{1,0:T(8,128)S(1)}, f32[256,512]{1,0:T(8,128)}, u32[]{:S(2)}) copy-start(f32[256,512]{1,0:T(8,128)} %param.17) | copy-start | bytes 1572868
  308.7 6.5 %copy-start.1 = (f32[256,512]{1,0:T(8,128)S(1)}, f32[256,512]{1,0:T(8,128)}, u32[]{:S(2)}) copy-start(f32[256,512]{1,0:T(8,128)} %param.16) | copy-start | bytes 1572868
  314.7 70.4 %all-gather.5.cloned.1.call-start = ((), (), s32[]{:S(2)}) async-start(), calls=%async_computation.4 | async-start | bytes 2359296 | tf_op jit(solution)/shard_map/all_gather | solution.py:58
Sparse Core Ops, SparseCore 0:
  82.8 77.2 all-gather.2
  314.9 40.1 reduce-scatter.1
  357.1 28.0 all-gather.4
where the time goes:
time: 425 us; the launch traced here: 422 us
  waiting for transfers between devices  148 us (35%)
  local copies, waits for them, and re-layouts  134 us (32%)
  other arithmetic  101 us (24%)
  matrix products  18.6 us (4%)
  between operations  14.5 us (3%)
  starting transfers between devices  6.83 us (2%)
    all_to_all x1, waiting for transfers between devices, shards(): lax.all_to_all(tokens, 'fsdp', split_axis=2, concat_axis=1, tiled=True)[0]  103 us
    unnamed x21, local copies, waits for them, and re-layouts  83.5 us
    unnamed x2, other arithmetic  43.5 us
    reduce_scatter x1, waiting for transfers between devices, shards(): lax.psum_scatter(fragment.astype(jnp.bfloat16), 'island', scatter_dimensi...  39.6 us
    add x4, other arithmetic, one_block(): return running + part  38.4 us
    dot_general x4, matrix products, one_block(): lax.dot_general(token_part, grads_part, (((0,), (0,)), ((), ())), preferr...  18.6 us
    scatter x2, local copies, waits for them, and re-layouts, shards(): shaped.at[:, heads, :].set(whole_base.reshape(rows, SYNC, HD))  17.3 us
    broadcast_in_dim x1, other arithmetic, shards(): moment_two.astype(jnp.bfloat16)[None]  15.2 us
  transfers between devices with their start and end apart: 4, of which 3 were waited for; matrix products, arithmetic and copies ran while one was open for 16% of the time, Pallas kernels for 0%

commit v1 on v0

--- a/solution.py
+++ b/solution.py
@@ -30,7 +30,11 @@
     rows = weights.shape[0]
     width = weights.shape[1]
     block = local_tokens.shape[0]
-    columns = lax.all_to_all(tokens, "fsdp", split_axis=2, concat_axis=1, tiled=True)[0]
+    _set_sides = lambda load: jnp.concatenate(
+        jax.lax.all_to_all(jnp.stack(jnp.split(load, jax.lax.axis_size("fsdp"), 2)), "fsdp", 0, 0),
+        1,
+    )
+    columns = _set_sides(tokens)[0]
     piece = lax.all_gather(cotangent, "fsdp", axis=1, tiled=True)
     blocks = piece.shape[1] // block
 

time: 425 us -> 343 us (0.81)
  other arithmetic: 101 us -> 59.6 us
  local copies, waits for them, and re-layouts: 134 us -> 93.4 us
    all_gather x1, waiting for transfers between devices: 0.01 us -> 55.7 us  [shards(): piece = lax.all_gather(cotangent, 'fsdp', axis=1, tiled=True)]
    all_to_all x1, waiting for transfers between devices: 103 us -> 47.5 us  [shards(): jax.lax.all_to_all(jnp.stack(jnp.split(load, jax.lax.axis_size('fsdp'), 2...]
    unnamed x2 -> x1, other arithmetic: 43.5 us -> 0.01 us
    unnamed x21 -> x16, local copies, waits for them, and re-layouts: 83.5 us -> 46.6 us
    all_to_all x1 -> x0, local copies, waits for them, and re-layouts: 6.19 us -> none  [shards(): lax.all_to_all(tokens, 'fsdp', split_axis=2, concat_axis=1, tiled=True)[0]]
  transfers between devices with their start and end apart: 4 -> 4, of which waited for: 3 -> 4; matrix products, arithmetic and copies ran while one was open for 16% -> 14% of each run, Pallas kernels for 0% -> 0%
where the time goes in v1:
time: 343 us; the launch traced here: 341 us
  waiting for transfers between devices  148 us (43%)
  local copies, waits for them, and re-layouts  93.4 us (27%)
  other arithmetic  59.6 us (17%)
  matrix products  18.6 us (5%)
  between operations  14.5 us (4%)
  starting transfers between devices  6.61 us (2%)
    all_gather x1, waiting for transfers between devices, shards(): piece = lax.all_gather(cotangent, 'fsdp', axis=1, tiled=True)  55.7 us
    all_to_all x1, waiting for transfers between devices, shards(): jax.lax.all_to_all(jnp.stack(jnp.split(load, jax.lax.axis_size('fsdp'), 2...  47.5 us
    unnamed x16, local copies, waits for them, and re-layouts  46.6 us
    reduce_scatter x1, waiting for transfers between devices, shards(): lax.psum_scatter(fragment.astype(jnp.bfloat16), 'island', scatter_dimensi...  39.8 us
    add x4, other arithmetic, one_block(): return running + part  38.4 us
    dot_general x4, matrix products, one_block(): lax.dot_general(token_part, grads_part, (((0,), (0,)), ((), ())), preferr...  18.6 us
    scatter x2, local copies, waits for them, and re-layouts, shards(): shaped.at[:, heads, :].set(whole_base.reshape(rows, SYNC, HD))  17.3 us
    broadcast_in_dim x1, other arithmetic, shards(): moment_two.astype(jnp.bfloat16)[None]  15.2 us
  transfers between devices with their start and end apart: 4, of which 4 were waited for; matrix products, arithmetic and copies ran while one was open for 14% of the time, Pallas kernels for 0%

profile of v1, /device:TPU:0, one launch (start us, length us, event | category | flops | bytes accessed | tf_op | source)
XLA Modules:
  0.0 340.9 jit_solution(6021229178864625108)
XLA Ops:
  7.2 2.8 slice_bitcast_fusion.3
  9.9 2.3 pad_maximum_fusion
  12.2 6.3 %all-to-all-start = ((bf16[4,1,256,2048]{3,2,1,0:T(8,128)(2,1)}), bf16[4,1,256,2048]{3,2,1,0:T(8,128)(2,1)}, u32[]{:S(2)}, u32[]{:S(2)}) async-start(bf16[4,1,256,2048]{3,2,1,0:T(8,128)(2,1)} %pad_maximum_fusion), calls=%async_computation | async-start | bytes 8388608 | tf_op jit(solution)/shard_map/all_to_all | solution.py:34
  19.3 9.3 %copy.15 = f32[1,2048,1024]{1,2,0:T(8,128)} copy(f32[1,2048,1024]{2,1,0:T(8,128)} %param.13) | data formatting | bytes 16777216 | tf_op args[2]
  28.6 6.6 %copy.16 = bf16[1,2048,1024]{1,2,0:T(8,128)(2,1)} copy(bf16[1,2048,1024]{2,1,0:T(8,128)(2,1)} %param.14) | data formatting | bytes 8388608 | tf_op args[3]
  35.2 6.4 %copy.18 = bf16[1,2048,1024]{1,2,0:T(8,128)(2,1)} copy(bf16[1,2048,1024]{2,1,0:T(8,128)(2,1)} %param.15) | data formatting | bytes 8388608 | tf_op args[4]
  42.5 55.7 %all-gather.3.cloned.1.call-done = bf16[1,1024,1024]{2,1,0:T(8,128)(2,1)} async-done(((bf16[1,256,1024]{2,1,0:T(8,128)(2,1)}), bf16[1,1024,1024]{2,1,0:T(8,128)(2,1)}) %all-gather.3.cloned.1.call-update) | async-done | bytes 2097168 | tf_op jit(solution)/shard_map/all_gather | solution.py:38
  98.2 47.5 %all-to-all-done = bf16[4,1,256,2048]{3,2,1,0:T(8,128)(2,1)} async-done(((bf16[4,1,256,2048]{3,2,1,0:T(8,128)(2,1)}), bf16[4,1,256,2048]{3,2,1,0:T(8,128)(2,1)}, u32[]{:S(2)}, u32[]{:S(2)}) %all-to-all-start) | async-done | bytes 4194336 | tf_op jit(solution)/shard_map/all_to_all | solution.py:34
  145.7 57.0 %while.14 = (s32[]{:T(128)}, f32[2048,1024]{1,0:T(8,128)}, bf16[1024,2048]{1,0:T(8,128)(2,1)}, bf16[1,1024,1024]{2,1,0:T(8,128)(2,1)}, s32[]{:T(128)}, /*index=5*/s32[]{:T(128)}, s32[]{:T(128)}, s32[]{:T(128)}) while((s32[]{:T(128)}, f32[2048,1024]{1,0:T(8,128)}, bf16[1024,2048]{1,0:T(8,128)(2,1)}, ...), condition=%wide.region_1.0_spmd.clone, body=%wide.region_0.0_spmd.clone.sunk | while | flops 1082130432 | bytes 26739852 | solution.py:50
  145.7 4.7 %convolution_convert_fusion.2 = bf16[2048,1024]{1,0:T(8,128)(2,1)} fusion(bf16[1024,2048]{1,0:T(8,128)(2,1)} %get-tuple-element.168, s32[]{:T(128)S(6)} %select_n.32, bf16[1,1024,1024]{2,1,0:T(8,128)(2,1)} %get-tuple-element.169), kind=kOutput, calls=%fused_computation.3.clone.1 | convolution fusion | flops 1075838976 | bytes 5768192 | tf_op jit(solution)/shard_map/while/body/eval_jaxpr/dot_general | solution.py:44
  150.4 7.8 %select_add_fusion.2 = f32[2048,1024]{1,0:T(8,128)} fusion(f32[2048,1024]{1,0:T(8,128)} %get-tuple-element.159, bf16[2048,1024]{1,0:T(8,128)(2,1)} %convolution_convert_fusion.2, pred[]{:T(512)S(6)} %compare.3), kind=kLoop, calls=%fused_computation.2.clone.1 | loop fusion | flops 6291456 | bytes 20971520 | tf_op jit(solution)/shard_map/while/body/eval_jaxpr/add | solution.py:48
  158.2 4.7 %convolution_convert_fusion.2 = bf16[2048,1024]{1,0:T(8,128)(2,1)} fusion(bf16[1024,2048]{1,0:T(8,128)(2,1)} %get-tuple-element.168, s32[]{:T(128)S(6)} %select_n.32, bf16[1,1024,1024]{2,1,0:T(8,128)(2,1)} %get-tuple-element.169), kind=kOutput, calls=%fused_computation.3.clone.1 | convolution fusion | flops 1075838976 | bytes 5768192 | tf_op jit(solution)/shard_map/while/body/eval_jaxpr/dot_general | solution.py:44
  162.8 10.2 %select_add_fusion.2 = f32[2048,1024]{1,0:T(8,128)} fusion(f32[2048,1024]{1,0:T(8,128)} %get-tuple-element.159, bf16[2048,1024]{1,0:T(8,128)(2,1)} %convolution_convert_fusion.2, pred[]{:T(512)S(6)} %compare.3), kind=kLoop, calls=%fused_computation.2.clone.1 | loop fusion | flops 6291456 | bytes 20971520 | tf_op jit(solution)/shard_map/while/body/eval_jaxpr/add | solution.py:48
  173.0 4.7 %convolution_convert_fusion.2 = bf16[2048,1024]{1,0:T(8,128)(2,1)} fusion(bf16[1024,2048]{1,0:T(8,128)(2,1)} %get-tuple-element.168, s32[]{:T(128)S(6)} %select_n.32, bf16[1,1024,1024]{2,1,0:T(8,128)(2,1)} %get-tuple-element.169), kind=kOutput, calls=%fused_computation.3.clone.1 | convolution fusion | flops 1075838976 | bytes 5768192 | tf_op jit(solution)/shard_map/while/body/eval_jaxpr/dot_general | solution.py:44
  177.7 10.2 %select_add_fusion.2 = f32[2048,1024]{1,0:T(8,128)} fusion(f32[2048,1024]{1,0:T(8,128)} %get-tuple-element.159, bf16[2048,1024]{1,0:T(8,128)(2,1)} %convolution_convert_fusion.2, pred[]{:T(512)S(6)} %compare.3), kind=kLoop, calls=%fused_computation.2.clone.1 | loop fusion | flops 6291456 | bytes 20971520 | tf_op jit(solution)/shard_map/while/body/eval_jaxpr/add | solution.py:48
  187.9 4.7 %convolution_convert_fusion.2 = bf16[2048,1024]{1,0:T(8,128)(2,1)} fusion(bf16[1024,2048]{1,0:T(8,128)(2,1)} %get-tuple-element.168, s32[]{:T(128)S(6)} %select_n.32, bf16[1,1024,1024]{2,1,0:T(8,128)(2,1)} %get-tuple-element.169), kind=kOutput, calls=%fused_computation.3.clone.1 | convolution fusion | flops 1075838976 | bytes 5768192 | tf_op jit(solution)/shard_map/while/body/eval_jaxpr/dot_general | solution.py:44
  192.5 10.2 %select_add_fusion.2 = f32[2048,1024]{1,0:T(8,128)} fusion(f32[2048,1024]{1,0:T(8,128)} %get-tuple-element.159, bf16[2048,1024]{1,0:T(8,128)(2,1)} %convolution_convert_fusion.2, pred[]{:T(512)S(6)} %compare.3), kind=kLoop, calls=%fused_computation.2.clone.1 | loop fusion | flops 6291456 | bytes 20971520 | tf_op jit(solution)/shard_map/while/body/eval_jaxpr/add | solution.py:48
  202.7 9.2 %copy.17 = f32[2048,1024]{0,1:T(8,128)} copy(f32[2048,1024]{1,0:T(8,128)} %get-tuple-element.84) | data formatting | bytes 16777216 | tf_op jit(solution)/shard_map/while | solution.py:50
  212.0 15.2 %fusion.9 = (bf16[1,2048,1024]{1,2,0:T(8,128)(2,1)}, f32[2048,1024]{0,1:T(8,128)}, bf16[1,2048,1024]{1,2,0:T(8,128)(2,1)}) fusion(f32[2048,1024]{0,1:T(8,128)} %copy.17, bf16[1,2048,1024]{1,2,0:T(8,128)(2,1)} %copy.18, bf16[1,2048,1024]{1,2,0:T(8,128)(2,1)} %copy.16, f32[1,2048,1024]{1,2,0:T(8,128)} %copy.15), kind=kLoop, calls=%fused_computation.17 | loop fusion | flops 35651584 | bytes 41943040 | tf_op jit(solution)/shard_map/broadcast_in_dim | solution.py:69
  227.2 4.2 %gather_fusion = bf16[4,2048,128]{1,2,0:T(8,128)(2,1)S(1)} fusion(f32[2048,8,128]{0,2,1:T(8,128)} %bitcast.57, s32[1024]{0:T(1024)S(1)} %pad_clamp_fusion), kind=kCustom, calls=%fused_computation | custom fusion | bytes 4194320 | tf_op jit(solution)/shard_map/jit(_take)/gather | solution.py:56
  231.4 1.8 fusion.11
  233.8 39.8 %reduce-scatter.2.cloned.1.call-done = bf16[256,512]{0,1:T(8,128)(2,1)} async-done(((bf16[2048,512]{0,1:T(8,128)(2,1)}), bf16[256,512]{0,1:T(8,128)(2,1)}) %reduce-scatter.2.cloned.1.call-update) | async-done | bytes 262160 | tf_op jit(solution)/shard_map/reduce_scatter | solution.py:58
  273.7 1.8 fusion.12
  275.5 9.2 %copy.25 = f32[2048,8,128]{2,0,1:T(8,128)} copy(f32[2048,8,128]{0,2,1:T(8,128)} %bitcast.58) | data formatting | bytes 16777216 | tf_op jit(solution)/shard_map/reshape | solution.py:55
  284.7 6.4 %copy.28 = bf16[1,2048,1024]{2,1,0:T(8,128)(2,1)} copy(bf16[1,2048,1024]{1,2,0:T(8,128)(2,1)} %get-tuple-element.119) | data formatting | bytes 8388608
  291.1 6.3 %copy.29 = bf16[1,2048,1024]{2,1,0:T(8,128)(2,1)} copy(bf16[1,2048,1024]{1,2,0:T(8,128)(2,1)} %get-tuple-element.117) | data formatting | bytes 8388608
  297.4 1.0 copy.30
  299.4 4.4 %all-gather.5.cloned.1.call-done = bf16[2048,512]{0,1:T(8,128)(2,1)} async-done(((bf16[256,512]{0,1:T(8,128)(2,1)}), bf16[2048,512]{0,1:T(8,128)(2,1)}) %all-gather.5.cloned.1.call-update) | async-done | bytes 2097168 | tf_op jit(solution)/shard_map/all_gather | solution.py:62
  303.8 4.1 %copy.24 = f32[2048,4,128]{2,0,1:T(8,128)} copy(bf16[2048,4,128]{0,2,1:T(8,128)(2,1)} %bitcast.61) | data formatting | bytes 6291456 | tf_op jit(solution)/shard_map/reshape | solution.py:65
  307.9 8.0 %scatter_fusion = f32[2048,8,128]{2,0,1:T(8,128)} fusion(f32[2048,8,128]{2,0,1:T(8,128)} %copy.25, s32[4]{0:T(128)S(1)} %get-tuple-element.116, f32[4,2048,128]{2,1,0:T(8,128)} %bitcast.60), kind=kCustom, calls=%fused_computation.1 | custom fusion | bytes 12582928 | tf_op jit(solution)/shard_map/scatter | solution.py:65
  316.0 9.2 %copy.26 = f32[2048,8,128]{0,2,1:T(8,128)} copy(f32[2048,8,128]{2,0,1:T(8,128)} %scatter_fusion) | data formatting | bytes 16777216 | tf_op jit(solution)/shard_map/scatter | solution.py:65
  325.2 9.2 %copy.27 = f32[1,2048,1024]{2,1,0:T(8,128)} copy(f32[1,2048,1024]{1,2,0:T(8,128)} %bitcast.59) | data formatting | bytes 16777216
  (19 shorter events, 2.6 us)
Async XLA Ops:
  12.2 133.5 %all-to-all-start = ((bf16[4,1,256,2048]{3,2,1,0:T(8,128)(2,1)}), bf16[4,1,256,2048]{3,2,1,0:T(8,128)(2,1)}, u32[]{:S(2)}, u32[]{:S(2)}) async-start(bf16[4,1,256,2048]{3,2,1,0:T(8,128)(2,1)} %pad_maximum_fusion), calls=%async_computation | async-start | bytes 8388608 | tf_op jit(solution)/shard_map/all_to_all | solution.py:34
  18.6 79.7 %all-gather.3.cloned.1.call-start = ((), (), s32[]{:S(2)}) async-start(), calls=%async_computation.2 | async-start | bytes 2621440 | tf_op jit(solution)/shard_map/all_gather | solution.py:38
  19.3 254.4 %reduce-scatter.2.cloned.1.call-start = ((), (), s32[]{:S(2)}) async-start(), calls=%async_computation.3 | async-start | bytes 2359296 | tf_op jit(solution)/shard_map/reduce_scatter | solution.py:58
  28.6 13.7 %copy-start.2 = (s32[8]{0:T(128)S(1)}, s32[8]{0:T(128)}, u32[]{:S(2)}) copy-start(s32[8]{0:T(128)} %param.18) | copy-start | bytes 100
  227.2 6.2 %copy-start = (f32[256,512]{1,0:T(8,128)S(1)}, f32[256,512]{1,0:T(8,128)}, u32[]{:S(2)}) copy-start(f32[256,512]{1,0:T(8,128)} %param.17) | copy-start | bytes 1572868
  227.2 6.5 %copy-start.1 = (f32[256,512]{1,0:T(8,128)S(1)}, f32[256,512]{1,0:T(8,128)}, u32[]{:S(2)}) copy-start(f32[256,512]{1,0:T(8,128)} %param.16) | copy-start | bytes 1572868
  233.2 70.6 %all-gather.5.cloned.1.call-start = ((), (), s32[]{:S(2)}) async-start(), calls=%async_computation.4 | async-start | bytes 2359296 | tf_op jit(solution)/shard_map/all_gather | solution.py:62
Sparse Core Ops, SparseCore 0:
  20.9 77.2 all-gather.2
  233.3 40.3 reduce-scatter.1
  275.7 28.0 all-gather.4
